TPU v7x, 512 devices: a whole 4x4x16 slice. The times are simulated.
512 devices in a mesh: dp: 8 (over z_hi, core), ctx: 64 (over x, z_lo, y).
Axes of the slice: x: 4, y: 4, z: 16 (z_hi: 4, z_lo: 4; z = z_hi * 4 + z_lo), core: 2. Of those that a mesh axis runs over, the one named last changes fastest.
Arguments:
- queries: bfloat16 [8, 2048, 8192], P('dp', None, 'ctx'), may hold values from -6 to 6
- keys: bfloat16 [8, 2048, 8192], P('dp', None, 'ctx'), may hold values from -6 to 6
- values: bfloat16 [8, 2048, 8192], P('dp', None, 'ctx'), may hold values from -6 to 6
- cotangent: bfloat16 [8, 2048, 8192], P('dp', None, 'ctx'), may hold values from -6 to 6
- residues: float32 [2048, 16], P(('dp', 'ctx')), may hold values from -1.5 to 1.5
- decays: float32 [2048, 16], P(('dp', 'ctx')), may hold values from 0.1 to 800
Outputs:
- mixed: bfloat16 [8, 2048, 8192], P('dp', None, 'ctx')
- grad_queries: bfloat16 [8, 2048, 8192], P('dp', None, 'ctx')
- grad_keys: bfloat16 [8, 2048, 8192], P('dp', None, 'ctx')
- grad_values: bfloat16 [8, 2048, 8192], P('dp', None, 'ctx')
- grad_residues: float32 [2048, 16], P(('dp', 'ctx'))
All inputs are finite; a program needn't handle non-finite values.
Results may differ from a plain program's by a relative error of at most 0.0057.
Values may be sent and summed in bfloat16 or wider, within the bound.
A program may use at most 64 MiB of HBM per device.

v0:
```python
import math

import jax
import jax.numpy as jnp
from jax import lax
from jax.sharding import PartitionSpec as P

exact_mode = lax.Precision.HIGHEST


def dft_tables(length):
    padded = 2 * length
    inner_len = 128
    outer_len = padded // inner_len
    half_len = outer_len // 2
    outer_freq = jnp.arange(outer_len, dtype=jnp.int32)[:, None]
    outer_pos = jnp.arange(half_len, dtype=jnp.int32)[None, :]
    outer_angle = (
        2.0 * math.pi / outer_len * (outer_freq * outer_pos % outer_len).astype(jnp.float32)
    )
    twist_pos = jnp.arange(inner_len, dtype=jnp.int32)[None, :]
    twist_angle = 2.0 * math.pi / padded * (outer_freq * twist_pos % padded).astype(jnp.float32)
    inner_pos = jnp.arange(inner_len, dtype=jnp.int32)
    inner_angle = (
        2.0
        * math.pi
        / inner_len
        * (inner_pos[:, None] * inner_pos[None, :] % inner_len).astype(jnp.float32)
    )
    outer_re = jnp.cos(outer_angle)
    outer_im = -jnp.sin(outer_angle)
    inner_re = jnp.cos(inner_angle)
    inner_im = -jnp.sin(inner_angle)
    outer_pair = jnp.stack([outer_re, outer_im])
    outer_joined = jnp.concatenate([outer_re, outer_im], axis=0)
    inner_fwd = jnp.concatenate(
        [
            jnp.concatenate([inner_re, inner_im], axis=1),
            jnp.concatenate([-inner_im, inner_re], axis=1),
        ],
        axis=0,
    )
    inner_inv = jnp.concatenate(
        [
            jnp.concatenate([inner_re, -inner_im], axis=1),
            jnp.concatenate([inner_im, inner_re], axis=1),
        ],
        axis=0,
    )
    return (
        outer_pair,
        outer_joined,
        jnp.cos(twist_angle),
        -jnp.sin(twist_angle),
        inner_fwd,
        inner_inv,
    )


def forward_transform(signal, tables):
    outer_pair, outer_joined, twist_re, twist_im, inner_fwd, inner_inv = tables
    row_count = signal.shape[0]
    blocks = signal.reshape(row_count, outer_pair.shape[2], 128)
    first = jnp.einsum("pkn,rnm->prkm", outer_pair, blocks, precision=exact_mode)
    turned_re = first[0] * twist_re - first[1] * twist_im
    turned_im = first[0] * twist_im + first[1] * twist_re
    joined = jnp.concatenate([turned_re, turned_im], axis=-1)
    return jnp.einsum("rkm,mj->rkj", joined, inner_fwd, precision=exact_mode)


def inverse_transform(spectrum, tables):
    outer_pair, outer_joined, twist_re, twist_im, inner_fwd, inner_inv = tables
    row_count = spectrum.shape[0]
    padded = outer_pair.shape[1] * 128
    middle = jnp.einsum("rkj,jm->rkm", spectrum, inner_inv, precision=exact_mode)
    mid_re = middle[..., :128]
    mid_im = middle[..., 128:]
    turned_re = mid_re * twist_re + mid_im * twist_im
    turned_im = mid_im * twist_re - mid_re * twist_im
    upper = jnp.concatenate([turned_re, turned_im], axis=1)
    lower = jnp.concatenate([turned_im, -turned_re], axis=1)
    stacked = jnp.stack([upper, lower])
    result = jnp.einsum("kn,qrkm->qrnm", outer_joined, stacked, precision=exact_mode)
    return result.reshape(2, row_count, -1) / padded


def modal_basis(decays, length):
    steps_t = jnp.arange(length, dtype=jnp.float32) / length
    mode_scale = jnp.sqrt(1.0 - jnp.exp(-2.0 * decays / length))
    mode_basis = jnp.exp(-decays[:, :, None] * steps_t[None, None, :])
    return (mode_scale, mode_basis)


def body(queries, keys, values, cotangent, residues, decays):
    n_dp = lax.axis_size("dp")
    n_ctx = lax.axis_size("ctx")
    seq_count, channels, tok_local = keys.shape
    chan_block = channels // (n_dp * n_ctx)
    length = tok_local * n_ctx
    tables = dft_tables(length)
    gated_in = (keys.astype(jnp.float32) * values.astype(jnp.float32)).astype(jnp.bfloat16)
    gated_grad = (cotangent.astype(jnp.float32) * queries.astype(jnp.float32)).astype(jnp.bfloat16)
    laid_in = gated_in.reshape(seq_count, n_dp, n_ctx, chan_block, tok_local)
    laid_grad = gated_grad.reshape(seq_count, n_dp, n_ctx, chan_block, tok_local)
    moved_in, moved_grad = (
        lax.all_to_all(
            lax.all_to_all(laid_in, "dp", split_axis=1, concat_axis=0, tiled=True),
            "ctx",
            split_axis=2,
            concat_axis=4,
            tiled=True,
        ),
        lax.all_to_all(
            lax.all_to_all(laid_grad, "dp", split_axis=1, concat_axis=0, tiled=True),
            "ctx",
            split_axis=2,
            concat_axis=4,
            tiled=True,
        ),
    )
    all_scale, all_basis = modal_basis(decays, length)
    filter_taps = jnp.einsum("cn,cnt->ct", residues * all_scale, all_basis, precision=exact_mode)
    row_count = moved_in.size // length
    seq_rows = row_count // chan_block
    filt = forward_transform(filter_taps, tables)
    filt_re = filt[..., :128]
    filt_im = filt[..., 128:]
    spec_shape = (seq_rows, chan_block) + filt.shape[1:]
    sig = forward_transform(
        moved_in.reshape(row_count, length).astype(jnp.float32), tables
    ).reshape(spec_shape)
    grd = forward_transform(
        moved_grad.reshape(row_count, length).astype(jnp.float32), tables
    ).reshape(spec_shape)
    sig_re = sig[..., :128]
    sig_im = sig[..., 128:]
    grd_re = grd[..., :128]
    grd_im = grd[..., 128:]
    packed_re = sig_re * filt_re - sig_im * filt_im - (filt_re * grd_im - filt_im * grd_re)
    packed_im = sig_re * filt_im + sig_im * filt_re + (filt_re * grd_re + filt_im * grd_im)
    packed = jnp.concatenate([packed_re, packed_im], axis=-1).reshape((row_count,) + filt.shape[1:])
    both = inverse_transform(packed, tables)
    convolved = both[0].astype(jnp.bfloat16)
    back_conv = both[1].astype(jnp.bfloat16)
    cross_re = jnp.sum(sig_re * grd_re + sig_im * grd_im, axis=0)
    cross_im = jnp.sum(sig_re * grd_im - sig_im * grd_re, axis=0)
    grad_taps = inverse_transform(jnp.concatenate([cross_re, cross_im], axis=-1), tables)[0]
    mode_grads = jnp.einsum("ct,cnt->cn", grad_taps, all_basis, precision=exact_mode)
    conv_back, grad_back = (
        lax.all_to_all(
            lax.all_to_all(
                convolved.reshape(seq_rows, 1, 1, chan_block, length),
                "dp",
                split_axis=0,
                concat_axis=1,
                tiled=True,
            ),
            "ctx",
            split_axis=4,
            concat_axis=2,
            tiled=True,
        ),
        lax.all_to_all(
            lax.all_to_all(
                back_conv.reshape(seq_rows, 1, 1, chan_block, length),
                "dp",
                split_axis=0,
                concat_axis=1,
                tiled=True,
            ),
            "ctx",
            split_axis=4,
            concat_axis=2,
            tiled=True,
        ),
    )
    grad_residues = mode_grads * all_scale / math.sqrt(seq_count * n_dp * length)
    conv_f = conv_back.reshape(seq_count, channels, tok_local).astype(jnp.float32)
    back_f = grad_back.reshape(seq_count, channels, tok_local).astype(jnp.float32)
    mixed = (queries.astype(jnp.float32) * conv_f).astype(jnp.bfloat16)
    grad_queries = (cotangent.astype(jnp.float32) * conv_f).astype(jnp.bfloat16)
    grad_keys = (back_f * values.astype(jnp.float32)).astype(jnp.bfloat16)
    grad_values = (back_f * keys.astype(jnp.float32)).astype(jnp.bfloat16)
    return (mixed, grad_queries, grad_keys, grad_values, grad_residues)


def solution(mesh):
    return jax.shard_map(
        body,
        mesh=mesh,
        in_specs=(
            P("dp", None, "ctx"),
            P("dp", None, "ctx"),
            P("dp", None, "ctx"),
            P("dp", None, "ctx"),
            P(("dp", "ctx"), None),
            P(("dp", "ctx"), None),
        ),
        out_specs=(
            P("dp", None, "ctx"),
            P("dp", None, "ctx"),
            P("dp", None, "ctx"),
            P("dp", None, "ctx"),
            P(("dp", "ctx"), None),
        ),
        check_vma=False,
    )
```

profile of v0, /device:TPU:1, one launch (start us, length us, event | category | flops | bytes accessed | tf_op | source)
XLA Modules:
  0.0 332.6 jit_solution(15153205872709470632)
XLA Ops:
  0.7 1.4 fusion.24
  3.0 16.6 %all-to-all-start.2 = ((bf16[1,8,64,4,128]{4,2,3,0,1:T(8,128)(2,1)}), bf16[1,8,64,4,128]{4,2,3,0,1:T(8,128)(2,1)S(1)}, u32[]{:S(2)}, u32[]{:S(2)}) async-start(bf16[1,8,64,4,128]{4,2,3,0,1:T(8,128)(2,1)} %copy.96), calls=%async_computation.2 | async-start | bytes 1048576 | tf_op jit(solution)/shard_map/all_to_all | solution.py:114
  20.7 21.3 %all-to-all-done.2 = bf16[1,8,64,4,128]{4,2,3,0,1:T(8,128)(2,1)S(1)} async-done(((bf16[1,8,64,4,128]{4,2,3,0,1:T(8,128)(2,1)}), bf16[1,8,64,4,128]{4,2,3,0,1:T(8,128)(2,1)S(1)}, u32[]{:S(2)}, u32[]{:S(2)}) %all-to-all-start.2) | async-done | bytes 524320 | tf_op jit(solution)/shard_map/all_to_all | solution.py:114
  42.0 13.9 %all-to-all-start = ((bf16[1,8,64,4,128]{4,2,3,0,1:T(8,128)(2,1)}), bf16[1,8,64,4,128]{4,2,3,0,1:T(8,128)(2,1)S(1)}, u32[]{:S(2)}, u32[]{:S(2)}) async-start(bf16[1,8,64,4,128]{4,2,3,0,1:T(8,128)(2,1)} %copy.85), calls=%async_computation | async-start | bytes 1048576 | tf_op jit(solution)/shard_map/all_to_all | solution.py:107
  57.1 26.2 %all-to-all-done = bf16[1,8,64,4,128]{4,2,3,0,1:T(8,128)(2,1)S(1)} async-done(((bf16[1,8,64,4,128]{4,2,3,0,1:T(8,128)(2,1)}), bf16[1,8,64,4,128]{4,2,3,0,1:T(8,128)(2,1)S(1)}, u32[]{:S(2)}, u32[]{:S(2)}) %all-to-all-start) | async-done | bytes 524320 | tf_op jit(solution)/shard_map/all_to_all | solution.py:107
  83.3 13.0 %all-to-all-start.3 = ((bf16[8,1,64,4,128]{4,3,0,1,2:T(4,128)(2,1)}), bf16[8,1,64,4,128]{4,3,0,1,2:T(4,128)(2,1)S(1)}, u32[]{:S(2)}, u32[]{:S(2)}) async-start(bf16[8,1,64,4,128]{4,3,0,1,2:T(4,128)(2,1)} %copy.97), calls=%async_computation.3 | async-start | bytes 1048576 | tf_op jit(solution)/shard_map/all_to_all | solution.py:113
  98.3 15.0 %all-to-all-done.3 = bf16[8,1,64,4,128]{4,3,0,1,2:T(4,128)(2,1)S(1)} async-done(((bf16[8,1,64,4,128]{4,3,0,1,2:T(4,128)(2,1)}), bf16[8,1,64,4,128]{4,3,0,1,2:T(4,128)(2,1)S(1)}, u32[]{:S(2)}, u32[]{:S(2)}) %all-to-all-start.3) | async-done | bytes 524320 | tf_op jit(solution)/shard_map/all_to_all | solution.py:113
  113.4 5.8 %all-to-all-start.1 = ((bf16[8,1,64,4,128]{4,3,0,1,2:T(4,128)(2,1)}), bf16[8,1,64,4,128]{4,3,0,1,2:T(4,128)(2,1)S(1)}, u32[]{:S(2)}, u32[]{:S(2)}) async-start(bf16[8,1,64,4,128]{4,3,0,1,2:T(4,128)(2,1)} %copy.86), calls=%async_computation.1 | async-start | bytes 1048576 | tf_op jit(solution)/shard_map/all_to_all | solution.py:106
  119.2 1.4 fusion.13
  124.1 3.8 %convolution_bitcast_fusion = f32[2,32,128,128]{2,3,1,0:T(8,128)} fusion(bf16[32,64,128,1]{2,1,0,3:T(8,128)(2,1)S(1)} %bitcast.160, f32[1,128,64]{1,2,0:T(8,128)S(1)} %get-tuple-element.39, f32[1,128,64]{1,2,0:T(8,128)S(1)} %get-tuple-element.40), kind=kOutput, calls=%fused_computation.15 | convolution fusion | flops 805322752 | bytes 4784128 | tf_op jit(solution)/shard_map/pkn,rnm->prkm/dot_general | solution.py:64
  127.9 8.1 %all-to-all-done.1 = bf16[8,1,64,4,128]{4,3,0,1,2:T(4,128)(2,1)S(1)} async-done(((bf16[8,1,64,4,128]{4,3,0,1,2:T(4,128)(2,1)}), bf16[8,1,64,4,128]{4,3,0,1,2:T(4,128)(2,1)S(1)}, u32[]{:S(2)}, u32[]{:S(2)}) %all-to-all-start.1) | async-done | bytes 524320 | tf_op jit(solution)/shard_map/all_to_all | solution.py:106
  136.2 1.9 convolution_bitcast_fusion.1
  138.3 1.9 multiply_subtract_fusion.2
  140.3 7.5 %fusion.4 = f32[32,128,256]{2,1,0:T(8,128)S(1)} fusion(f32[32,128,128]{1,2,0:T(8,128)S(1)} %get-tuple-element.17, f32[32,128,128]{1,2,0:T(8,128)S(1)} %get-tuple-element.16, f32[128,128]{1,0:T(8,128)S(1)} %get-tuple-element.42, f32[128,128]{1,0:T(8,128)S(1)} %get-tuple-element.41, f32[128,128]{1,0:T(8,128)S(1)} %fusion.81), kind=kOutput, calls=%fused_computation.4 | convolution fusion | flops 3222470656 | bytes 8585216 | tf_op jit(solution)/shard_map/rkm,mj->rkj/dot_general | solution.py:68
  147.7 7.3 %fusion.8 = f32[32,128,256]{2,1,0:T(8,128)S(1)} fusion(f32[32,128,128]{1,2,0:T(8,128)S(1)} %get-tuple-element.35, f32[32,128,128]{1,2,0:T(8,128)S(1)} %get-tuple-element.36, f32[128,128]{1,0:T(8,128)S(1)} %get-tuple-element.42, f32[128,128]{1,0:T(8,128)S(1)} %get-tuple-element.41, f32[128,128]{1,0:T(8,128)S(1)} %fusion.81), kind=kOutput, calls=%fused_computation.8 | convolution fusion | flops 3222470656 | bytes 8585216 | tf_op jit(solution)/shard_map/rkm,mj->rkj/dot_general | solution.py:68
  155.0 2.0 add_reduce_fusion
  157.4 4.4 %fusion.46 = f32[32,128,256]{1,2,0:T(8,128)S(1)} fusion(f32[32,128,256]{2,1,0:T(8,128)S(1)} %bitcast.154, f32[128,128]{1,0:T(8,128)S(1)} %get-tuple-element.42, f32[128,128]{1,0:T(8,128)S(1)} %fusion.81, f32[128,128]{1,0:T(8,128)S(1)} %get-tuple-element.41), kind=kOutput, calls=%fused_computation.82 | convolution fusion | flops 3221422080 | bytes 8585216 | tf_op jit(solution)/shard_map/rkj,jm->rkm/dot_general | solution.py:75
  163.4 8.3 %fusion.16 = bf16[2,32,64,128]{3,2,1,0:T(8,128)(2,1)S(1)} fusion(f32[1,32,256,128]{2,3,1,0:T(8,128)S(1)} %get-tuple-element.21, f32[1,32,256,128]{2,3,1,0:T(8,128)S(1)} %get-tuple-element.20, f32[128,64]{0,1:T(8,128)S(1)} %copy-done.5, f32[128,64]{0,1:T(8,128)S(1)} %copy-done.6), kind=kOutput, calls=%fused_computation.35 | convolution fusion | flops 1613774848 | bytes 9502720 | tf_op jit(solution)/shard_map/kn,qrkm->qrnm/dot_general | solution.py:83
  172.7 6.0 %all-to-all-start.6 = ((bf16[8,1,1,4,8192]{4,3,2,1,0:T(4,128)(2,1)}), bf16[8,1,1,4,8192]{4,3,2,1,0:T(4,128)(2,1)S(1)}, u32[]{:S(2)}, u32[]{:S(2)}) async-start(bf16[8,1,1,4,8192]{4,3,2,1,0:T(4,128)(2,1)} %bitcast.44), calls=%async_computation.6 | async-start | bytes 1048576 | tf_op jit(solution)/shard_map/all_to_all | solution.py:164
  179.6 23.8 %all-to-all-done.6 = bf16[8,1,1,4,8192]{4,3,2,1,0:T(4,128)(2,1)S(1)} async-done(((bf16[8,1,1,4,8192]{4,3,2,1,0:T(4,128)(2,1)}), bf16[8,1,1,4,8192]{4,3,2,1,0:T(4,128)(2,1)S(1)}, u32[]{:S(2)}, u32[]{:S(2)}) %all-to-all-start.6) | async-done | bytes 524320 | tf_op jit(solution)/shard_map/all_to_all | solution.py:164
  203.4 10.4 %all-to-all-start.4 = ((bf16[8,1,1,4,8192]{4,3,2,1,0:T(4,128)(2,1)}), bf16[8,1,1,4,8192]{4,3,2,1,0:T(4,128)(2,1)S(1)}, u32[]{:S(2)}, u32[]{:S(2)}) async-start(bf16[8,1,1,4,8192]{4,3,2,1,0:T(4,128)(2,1)} %bitcast.38), calls=%async_computation.4 | async-start | bytes 1048576 | tf_op jit(solution)/shard_map/all_to_all | solution.py:151
  213.8 8.2 %copy.108 = bf16[1,8,1,4,8192]{1,3,2,0,4:T(4,128)(2,1)} copy(bf16[1,8,1,4,8192]{4,3,1,2,0:T(4,128)(2,1)S(1)} %bitcast.158) | data formatting | bytes 1048576 | tf_op jit(solution)/shard_map/all_to_all | solution.py:164
  222.0 11.2 %reshape.269 = bf16[64,2,2048]{2,1,0:T(2,128)(2,1)} reshape(bf16[8192,1,1,4,8]{4,3,2,1,0:T(4,128)(2,1)} %bitcast.148) | data formatting | bytes 1048576
  233.2 18.3 %all-to-all-start.7 = ((bf16[64,2,2048]{2,1,0:T(2,128)(2,1)}), bf16[64,2,2048]{2,1,0:T(2,128)(2,1)S(1)}, u32[]{:S(2)}, u32[]{:S(2)}) async-start(bf16[64,2,2048]{2,1,0:T(2,128)(2,1)} %reshape.269), calls=%async_computation.7 | async-start | bytes 1048576 | tf_op jit(solution)/shard_map/all_to_all | solution.py:163
  251.5 8.3 %copy.105 = bf16[1,8,1,4,8192]{1,3,2,0,4:T(4,128)(2,1)} copy(bf16[1,8,1,4,8192]{4,3,1,2,0:T(4,128)(2,1)S(1)} %bitcast.157) | data formatting | bytes 1048576 | tf_op jit(solution)/shard_map/all_to_all | solution.py:151
  259.8 11.2 %reshape.267 = bf16[64,2,2048]{2,1,0:T(2,128)(2,1)} reshape(bf16[8192,1,1,4,8]{4,3,2,1,0:T(4,128)(2,1)} %bitcast.149) | data formatting | bytes 1048576
  271.0 10.1 %all-to-all-start.5 = ((bf16[64,2,2048]{2,1,0:T(2,128)(2,1)}), bf16[64,2,2048]{2,1,0:T(2,128)(2,1)S(1)}, u32[]{:S(2)}, u32[]{:S(2)}) async-start(bf16[64,2,2048]{2,1,0:T(2,128)(2,1)} %reshape.267), calls=%async_computation.5 | async-start | bytes 1048576 | tf_op jit(solution)/shard_map/all_to_all | solution.py:150
  283.1 2.9 fusion.12
  286.6 11.0 %reshape.270 = bf16[8192,1,1,4,8]{4,3,2,1,0:T(4,128)(2,1)} reshape(bf16[64,2,2048]{2,1,0:T(2,128)(2,1)S(1)} %all-to-all-done.7) | data formatting | bytes 1048576
  297.5 10.7 %copy.109 = f32[1,8,1,4,64,128]{5,3,4,1,2,0:T(4,128)S(1)} copy(bf16[1,8,1,4,64,128]{1,3,5,4,2,0:T(4,128)(2,1)} %bitcast.150) | data formatting | bytes 1572864 | tf_op jit(solution)/shard_map/convert_element_type | solution.py:179
  309.4 11.0 %reshape.268 = bf16[8192,1,1,4,8]{4,3,2,1,0:T(4,128)(2,1)} reshape(bf16[64,2,2048]{2,1,0:T(2,128)(2,1)S(1)} %all-to-all-done.5) | data formatting | bytes 1048576
  320.4 10.8 %copy.106 = f32[1,8,1,4,64,128]{5,3,4,1,2,0:T(4,128)S(1)} copy(bf16[1,8,1,4,64,128]{1,3,5,4,2,0:T(4,128)(2,1)} %bitcast.151) | data formatting | bytes 1572864 | tf_op jit(solution)/shard_map/convert_element_type | solution.py:178
  (61 shorter events, 17.9 us)
Async XLA Ops:
  0.6 19.0 %copy-start.2 = (bf16[1,2048,128]{2,1,0:T(8,128)(2,1)S(1)}, bf16[1,2048,128]{2,1,0:T(8,128)(2,1)}, u32[]{:S(2)}) copy-start(bf16[1,2048,128]{2,1,0:T(8,128)(2,1)} %param.7) | copy-start | bytes 1572868
  0.6 19.0 %copy-start.1 = (bf16[1,2048,128]{2,1,0:T(8,128)(2,1)S(1)}, bf16[1,2048,128]{2,1,0:T(8,128)(2,1)}, u32[]{:S(2)}) copy-start(bf16[1,2048,128]{2,1,0:T(8,128)(2,1)} %param.8) | copy-start | bytes 1572868
  3.0 39.0 %all-to-all-start.2 = ((bf16[1,8,64,4,128]{4,2,3,0,1:T(8,128)(2,1)}), bf16[1,8,64,4,128]{4,2,3,0,1:T(8,128)(2,1)S(1)}, u32[]{:S(2)}, u32[]{:S(2)}) async-start(bf16[1,8,64,4,128]{4,2,3,0,1:T(8,128)(2,1)} %copy.96), calls=%async_computation.2 | async-start | bytes 1048576 | tf_op jit(solution)/shard_map/all_to_all | solution.py:114
  42.0 41.3 %all-to-all-start = ((bf16[1,8,64,4,128]{4,2,3,0,1:T(8,128)(2,1)}), bf16[1,8,64,4,128]{4,2,3,0,1:T(8,128)(2,1)S(1)}, u32[]{:S(2)}, u32[]{:S(2)}) async-start(bf16[1,8,64,4,128]{4,2,3,0,1:T(8,128)(2,1)} %copy.85), calls=%async_computation | async-start | bytes 1048576 | tf_op jit(solution)/shard_map/all_to_all | solution.py:107
  55.9 63.2 %copy-start.9 = (f32[4,16]{1,0:T(4,128)S(1)}, f32[4,16]{1,0:T(4,128)}, u32[]{:S(2)}) copy-start(f32[4,16]{1,0:T(4,128)} %param.11) | copy-start | bytes 772
  55.9 63.2 %copy-start.10 = (f32[4,16]{1,0:T(4,128)S(1)}, f32[4,16]{1,0:T(4,128)}, u32[]{:S(2)}) copy-start(f32[4,16]{1,0:T(4,128)} %param.10) | copy-start | bytes 772
  83.3 30.0 %all-to-all-start.3 = ((bf16[8,1,64,4,128]{4,3,0,1,2:T(4,128)(2,1)}), bf16[8,1,64,4,128]{4,3,0,1,2:T(4,128)(2,1)S(1)}, u32[]{:S(2)}, u32[]{:S(2)}) async-start(bf16[8,1,64,4,128]{4,3,0,1,2:T(4,128)(2,1)} %copy.97), calls=%async_computation.3 | async-start | bytes 1048576 | tf_op jit(solution)/shard_map/all_to_all | solution.py:113
  97.1 23.4 %copy-start.7 = (f32[8192]{0:T(1024)}, f32[8192]{0:T(1024)S(1)}, u32[]{:S(2)}) copy-start(f32[8192]{0:T(1024)S(1)} %iota_multiply_fusion.1) | copy-start | bytes 98308
  113.4 22.6 %all-to-all-start.1 = ((bf16[8,1,64,4,128]{4,3,0,1,2:T(4,128)(2,1)}), bf16[8,1,64,4,128]{4,3,0,1,2:T(4,128)(2,1)S(1)}, u32[]{:S(2)}, u32[]{:S(2)}) async-start(bf16[8,1,64,4,128]{4,3,0,1,2:T(4,128)(2,1)} %copy.86), calls=%async_computation.1 | async-start | bytes 1048576 | tf_op jit(solution)/shard_map/all_to_all | solution.py:106
  136.2 2.2 copy-start
  162.6 0.8 copy-start.5
  162.6 0.8 copy-start.6
  172.7 30.7 %all-to-all-start.6 = ((bf16[8,1,1,4,8192]{4,3,2,1,0:T(4,128)(2,1)}), bf16[8,1,1,4,8192]{4,3,2,1,0:T(4,128)(2,1)S(1)}, u32[]{:S(2)}, u32[]{:S(2)}) async-start(bf16[8,1,1,4,8192]{4,3,2,1,0:T(4,128)(2,1)} %bitcast.44), calls=%async_computation.6 | async-start | bytes 1048576 | tf_op jit(solution)/shard_map/all_to_all | solution.py:164
  203.4 29.8 %all-to-all-start.4 = ((bf16[8,1,1,4,8192]{4,3,2,1,0:T(4,128)(2,1)}), bf16[8,1,1,4,8192]{4,3,2,1,0:T(4,128)(2,1)S(1)}, u32[]{:S(2)}, u32[]{:S(2)}) async-start(bf16[8,1,1,4,8192]{4,3,2,1,0:T(4,128)(2,1)} %bitcast.38), calls=%async_computation.4 | async-start | bytes 1048576 | tf_op jit(solution)/shard_map/all_to_all | solution.py:151
  233.2 37.7 %all-to-all-start.7 = ((bf16[64,2,2048]{2,1,0:T(2,128)(2,1)}), bf16[64,2,2048]{2,1,0:T(2,128)(2,1)S(1)}, u32[]{:S(2)}, u32[]{:S(2)}) async-start(bf16[64,2,2048]{2,1,0:T(2,128)(2,1)} %reshape.269), calls=%async_computation.7 | async-start | bytes 1048576 | tf_op jit(solution)/shard_map/all_to_all | solution.py:163
  271.0 38.4 %all-to-all-start.5 = ((bf16[64,2,2048]{2,1,0:T(2,128)(2,1)}), bf16[64,2,2048]{2,1,0:T(2,128)(2,1)S(1)}, u32[]{:S(2)}, u32[]{:S(2)}) async-start(bf16[64,2,2048]{2,1,0:T(2,128)(2,1)} %reshape.267), calls=%async_computation.5 | async-start | bytes 1048576 | tf_op jit(solution)/shard_map/all_to_all | solution.py:150
  281.8 1.2 copy-start.8
  320.4 10.8 %copy-start.3 = (bf16[1,2048,128]{2,1,0:T(8,128)(2,1)S(1)}, bf16[1,2048,128]{2,1,0:T(8,128)(2,1)}, u32[]{:S(2)}) copy-start(bf16[1,2048,128]{2,1,0:T(8,128)(2,1)} %param.6) | copy-start | bytes 1572868
  320.4 10.8 %copy-start.4 = (bf16[1,2048,128]{2,1,0:T(8,128)(2,1)S(1)}, bf16[1,2048,128]{2,1,0:T(8,128)(2,1)}, u32[]{:S(2)}) copy-start(bf16[1,2048,128]{2,1,0:T(8,128)(2,1)} %param.9) | copy-start | bytes 1572868
where the time goes:
time: 339 us; the launch traced here: 333 us
  waiting for transfers between devices  94.5 us (28%)
  starting transfers between devices  94 us (28%)
  local copies, waits for them, and re-layouts  89.6 us (26%)
  matrix products  40.7 us (12%)
  other arithmetic  12.5 us (4%)
    unnamed x26, local copies, waits for them, and re-layouts  44.8 us
    all_to_all x1, waiting for transfers between devices, body(): lax.all_to_all(laid_in, 'dp', split_axis=1, concat_axis=0, tiled=True)  26.2 us
    all_to_all x1, waiting for transfers between devices, body(): lax.all_to_all(back_conv.reshape(seq_rows, 1, 1, chan_block, length), 'dp...  23.8 us
    all_to_all x1, waiting for transfers between devices, body(): lax.all_to_all(laid_grad, 'dp', split_axis=1, concat_axis=0, tiled=True)  21.3 us
    all_to_all x1, starting transfers between devices, body(): lax.all_to_all(lax.all_to_all(back_conv.reshape(seq_rows, 1, 1, chan_bloc...  18.3 us
    all_to_all x1, starting transfers between devices, body(): lax.all_to_all(laid_grad, 'dp', split_axis=1, concat_axis=0, tiled=True)  16.6 us
    dot_general x3, matrix products, forward_transform(): return jnp.einsum('rkm,mj->rkj', joined, inner_fwd, precision=exact_mode)  15.7 us
    all_to_all x1, waiting for transfers between devices, body(): lax.all_to_all(lax.all_to_all(laid_grad, 'dp', split_axis=1, concat_axis=...  15 us
  transfers between devices with their start and end apart: 8, of which 5 were waited for; matrix products, arithmetic and copies ran while one was open for 24% of the time, Pallas kernels for 0%

commit v1 on v0

v1 whole, which is shorter than its diff:
```python
import math

import jax
import jax.numpy as jnp
from jax import lax
from jax.sharding import PartitionSpec as P

exact_mode = lax.Precision.HIGHEST


def shift_along(x, axis, n, step):
    if step > 0:
        pairs = [(i, i + step) for i in range(n - step)]
    else:
        pairs = [(i, i + step) for i in range(-step, n)]
    return lax.ppermute(x, axis, perm=pairs)


def chunk_scan(state, chunk_decay, axis, n, direction):
    carry = shift_along(state, axis, n, direction)
    hop = 1
    while hop < n:
        carry = carry + jnp.exp(-chunk_decay * hop) * shift_along(carry, axis, n, direction * hop)
        hop *= 2
    return carry


def body(queries, keys, values, cotangent, residues, decays):
    n_dp = lax.axis_size("dp")
    n_ctx = lax.axis_size("ctx")
    seq_count, channels, chunk = keys.shape
    order = residues.shape[1]
    length = chunk * n_ctx
    f32 = jnp.float32

    params = lax.all_gather(
        jnp.concatenate([residues, decays], axis=1), ("dp", "ctx"), axis=0, tiled=True
    )
    dec = params[:, order:]
    scale = jnp.sqrt(1.0 - jnp.exp(-2.0 * dec / length))
    weight = params[:, :order] * scale

    gated_in = (keys.astype(f32) * values.astype(f32)).astype(jnp.bfloat16)
    gated_grad = (cotangent.astype(f32) * queries.astype(f32)).astype(jnp.bfloat16)
    g = gated_in[0].astype(f32)
    gg = gated_grad[0].astype(f32)

    pos = jnp.arange(chunk, dtype=f32)
    mid = chunk // 2
    dk = dec[:, :, None]
    grow = jnp.exp(dk * ((pos - mid) / length))
    shrink = jnp.exp(-dk * ((pos - mid) / length))
    upper = (pos[:, None] <= pos[None, :]).astype(f32)
    lower = (pos[:, None] >= pos[None, :]).astype(f32)

    end_fwd = jnp.sum(g[:, None, :] * jnp.exp(-dk * ((chunk - 1 - pos) / length)), axis=-1)
    start_bwd = jnp.sum(gg[:, None, :] * jnp.exp(-dk * (pos / length)), axis=-1)
    chunk_decay = dec * (chunk / length)
    carry_fwd = chunk_scan(end_fwd, chunk_decay, "ctx", n_ctx, 1)
    carry_bwd = chunk_scan(start_bwd, chunk_decay, "ctx", n_ctx, -1)

    fwd_state = shrink * jnp.einsum(
        "dnc,ct->dnt", g[:, None, :] * grow, upper, precision=exact_mode
    )
    bwd_state = grow * jnp.einsum(
        "dnc,ct->dnt", gg[:, None, :] * shrink, lower, precision=exact_mode
    )
    conv_intra = jnp.sum(weight[:, :, None] * fwd_state, axis=1)
    back_intra = jnp.sum(weight[:, :, None] * bwd_state, axis=1)
    cross_intra = jnp.sum(gg[:, None, :] * fwd_state, axis=-1)

    lead_fwd = jnp.exp(-dk * ((pos + 1) / length))
    lead_bwd = jnp.exp(-dk * ((chunk - pos) / length))
    conv_full = conv_intra + jnp.sum((weight * carry_fwd)[:, :, None] * lead_fwd, axis=1)
    back_full = back_intra + jnp.sum((weight * carry_bwd)[:, :, None] * lead_bwd, axis=1)
    cross = cross_intra + carry_fwd * jnp.sum(gg[:, None, :] * lead_fwd, axis=-1)

    total = lax.psum_scatter(cross, ("dp", "ctx"), scatter_dimension=0, tiled=True)
    own_scale = jnp.sqrt(1.0 - jnp.exp(-2.0 * decays / length))
    grad_residues = total * own_scale / math.sqrt(seq_count * n_dp * length)

    conv_f = conv_full.astype(jnp.bfloat16).astype(f32)[None]
    back_f = back_full.astype(jnp.bfloat16).astype(f32)[None]
    mixed = (queries.astype(f32) * conv_f).astype(jnp.bfloat16)
    grad_queries = (cotangent.astype(f32) * conv_f).astype(jnp.bfloat16)
    grad_keys = (back_f * values.astype(f32)).astype(jnp.bfloat16)
    grad_values = (back_f * keys.astype(f32)).astype(jnp.bfloat16)
    return (mixed, grad_queries, grad_keys, grad_values, grad_residues)


def solution(mesh):
    return jax.shard_map(
        body,
        mesh=mesh,
        in_specs=(
            P("dp", None, "ctx"),
            P("dp", None, "ctx"),
            P("dp", None, "ctx"),
            P("dp", None, "ctx"),
            P(("dp", "ctx"), None),
            P(("dp", "ctx"), None),
        ),
        out_specs=(
            P("dp", None, "ctx"),
            P("dp", None, "ctx"),
            P("dp", None, "ctx"),
            P("dp", None, "ctx"),
            P(("dp", "ctx"), None),
        ),
        check_vma=False,
    )
```

time: 339 us -> 1970 us (5.81)
  blocking collectives: 0 us -> 1330 us
  waiting for transfers between devices: 94.5 us -> 526 us
  local copies, waits for them, and re-layouts: 89.6 us -> 9.73 us
  starting transfers between devices: 94 us -> 33.5 us
    all_gather x0 -> x1, blocking collectives: none -> 1330 us  [body(): lax.all_gather(jnp.concatenate([residues, decays], axis=1), ('dp', 'ctx')...]
    unnamed x0 -> x2, waiting for transfers between devices: none -> 493 us
    all_to_all x8 -> x0, waiting for transfers between devices: 94.5 us -> none  [the longest x1 26.2 us: body(): lax.all_to_all(laid_in, 'dp', split_axis=1, concat_axis=0, tiled=True)]
    all_to_all x8 -> x0, starting transfers between devices: 94 us -> none  [the longest x1 18.3 us: body(): lax.all_to_all(lax.all_to_all(back_conv.reshape(seq_rows, 1, 1, chan_bloc...]
    unnamed x26 -> x34, local copies, waits for them, and re-layouts: 44.8 us -> 8.03 us
    ppermute x0 -> x14, starting transfers between devices: none -> 33.5 us  [shift_along(): return lax.ppermute(x, axis, perm=pairs)]
    ppermute x0 -> x14, waiting for transfers between devices: none -> 33.2 us  [shift_along(): return lax.ppermute(x, axis, perm=pairs)]
    convert_element_type x4 -> x0, local copies, waits for them, and re-layouts: 23.3 us -> none  [the longest x1 10.8 us: body(): conv_back.reshape(seq_count, channels, tok_local).astype(jnp.float32)]
  transfers between devices with their start and end apart: 8 -> 15, of which waited for: 5 -> 13; matrix products, arithmetic and copies ran while one was open for 24% -> 1% of each run, Pallas kernels for 0% -> 0%
where the time goes in v1:
time: 1970 us
  blocking collectives  1330 us (68%)
  waiting for transfers between devices  526 us (27%)
  matrix products  44.8 us (2%)
  starting transfers between devices  33.5 us (2%)
    all_gather x1, blocking collectives, body(): lax.all_gather(jnp.concatenate([residues, decays], axis=1), ('dp', 'ctx')...  1330 us
    unnamed x2, waiting for transfers between devices  493 us
  transfers between devices with their start and end apart: 15, of which 13 were waited for; matrix products, arithmetic and copies ran while one was open for 1% of the time, Pallas kernels for 0%

profile of v1, /device:TPU:1, one launch (start us, length us, event | category | flops | bytes accessed | tf_op | source)
XLA Modules:
  0.0 1972.8 jit_solution(14904116960434394480)
XLA Ops:
  8.0 1328.5 %all-gather = f32[512,4,32]{2,1,0:T(4,128)S(1)} all-gather(f32[1,4,32]{2,1,0:T(4,128)S(1)} %maximum_bitcast_fusion), channel_id=1, replica_groups=mesh['dp'=8,'ctx'=64] {'dp','ctx'}, dimensions={0}, use_global_device_ids=true | all-gather | bytes 262656 | tf_op jit(solution)/shard_map/all_gather | solution.py:36
  1338.6 3.0 multiply_reduce_fusion.6
  1341.6 1.4 collective-permute-start
  1343.0 1.9 collective-permute-done
  1344.9 3.8 collective-permute-start.1
  1348.7 1.9 collective-permute-done.1
  1350.7 4.1 collective-permute-start.2
  1354.8 1.9 collective-permute-done.2
  1356.8 3.5 collective-permute-start.3
  1360.3 1.9 collective-permute-done.3
  1362.2 3.5 collective-permute-start.4
  1367.7 3.5 collective-permute-start.5
  1373.2 4.3 collective-permute-start.6
  1379.2 1.7 fusion.30
  1380.9 27.1 %multiply_reduce_fusion = (f32[2048,16]{0,1:T(8,128)S(1)}, f32[2048,16]{0,1:T(8,128)S(1)}, f32[2048,128]{0,1:T(8,128)}, f32[2048,16]{0,1:T(8,128)S(1)}, f32[2048,128]{0,1:T(8,128)}) fusion(f32[2048,128]{0,1:T(8,128)} %fusion.22, f32[128]{0:T(128)S(1)} %get-tuple-element.33, f32[2048,16]{0,1:T(8,128)} %copy-done.9, f32[128]{0:T(128)S(1)} %get-tuple-element.32, ...), kind=kOutput, calls=%fused_computation | convolution fusion | flops 6508953600 | bytes 5113344 | tf_op jit(solution)/shard_map/dnc,ct->dnt/dot_general | solution.py:62
  1408.1 1.4 collective-permute-start.7
  1409.5 4.4 collective-permute-done.7
  1413.9 1.3 collective-permute-start.8
  1415.2 4.4 collective-permute-done.8
  1419.6 1.6 multiply_add_fusion
  1421.2 1.3 collective-permute-start.9
  1422.5 6.2 collective-permute-done.9
  1429.8 1.3 collective-permute-start.10
  1431.1 17.7 multiply_reduce_fusion.4
  1448.8 1.3 collective-permute-start.11
  1450.4 5.1 collective-permute-done.11
  1455.5 1.3 collective-permute-start.12
  1458.9 1.4 copy.43
  1460.3 3.4 collective-permute-done.12
  1463.8 1.5 collective-permute-start.13
  1465.3 493.2 %all-reduce.3.cloned.1.call-done = f32[2048,16]{1,0:T(8,128)} async-done(((f32[2048,16]{1,0:T(8,128)}), f32[2048,16]{1,0:T(8,128)}) %all-reduce.3.cloned.1.call-update) | async-done | bytes 131088
  1960.8 2.8 multiply_reduce_fusion.2
  (65 shorter events, 16.7 us)
Async XLA Ops:
  7.2 1951.4 %all-reduce.3.cloned.1.call-start = ((), (), s32[]{:S(2)}) async-start(), calls=%async_computation | async-start | bytes 2097152
  1336.8 1.0 copy-start.5
  1337.1 1.1 copy-start.6
  1337.8 0.7 copy-start.9
  1338.6 3.0 copy-start.3
  1341.6 24.2 %copy-start.7 = (bf16[1,2048,128]{2,1,0:T(8,128)(2,1)S(1)}, bf16[1,2048,128]{2,1,0:T(8,128)(2,1)}, u32[]{:S(2)}) copy-start(bf16[1,2048,128]{2,1,0:T(8,128)(2,1)} %param.9) | copy-start | bytes 1572868
  1341.6 3.4 collective-permute-start
  1344.9 5.7 collective-permute-start.1
  1350.7 6.0 collective-permute-start.2
  1356.8 5.4 collective-permute-start.3
  1362.2 5.4 collective-permute-start.4
  1367.7 5.4 collective-permute-start.5
  1373.2 6.0 collective-permute-start.6
  1379.2 28.8 %copy-start.8 = (f32[2048,16]{0,1:T(8,128)}, f32[2048,16]{0,1:T(8,128)S(1)}, u32[]{:S(2)}) copy-start(f32[2048,16]{0,1:T(8,128)S(1)} %collective-permute-done.6) | copy-start | bytes 393220
  1408.1 23.0 %copy-start.4 = (f32[2048,128]{0,1:T(8,128)S(1)}, f32[2048,128]{0,1:T(8,128)}, u32[]{:S(2)}) copy-start(f32[2048,128]{0,1:T(8,128)} %fusion.22) | copy-start | bytes 3145732
  1408.1 5.8 collective-permute-start.7
  1413.9 5.7 collective-permute-start.8
  1421.2 7.5 collective-permute-start.9
  1429.8 19.0 collective-permute-start.10
  1431.1 19.0 copy-start.1
  1431.1 19.0 copy-start.2
  1448.8 6.6 collective-permute-start.11
  1455.5 8.3 collective-permute-start.12
  1460.3 498.3 %copy-start.11 = (f32[4,16]{1,0:T(4,128)S(1)}, f32[4,16]{1,0:T(4,128)}, u32[]{:S(2)}) copy-start(f32[4,16]{1,0:T(4,128)} %param.11) | copy-start | bytes 772
  1460.3 500.5 %copy-start.10 = (f32[2048,16]{0,1:T(8,128)S(1)}, f32[2048,16]{0,1:T(8,128)}, u32[]{:S(2)}) copy-start(f32[2048,16]{0,1:T(8,128)} %copy-done.9) | copy-start | bytes 393220
  1463.8 496.0 %collective-permute-start.13 = (f32[2048,16]{0,1:T(8,128)S(1)}, f32[2048,16]{0,1:T(8,128)S(1)}, u32[]{:S(2)}, u32[]{:S(2)}) collective-permute-start(f32[2048,16]{0,1:T(8,128)S(1)} %multiply_add_fusion.1), channel_id=1, source_target_pairs={{32,0},{33,1},{34,2},{35,3},{36,4},{37,5},{38,6},{39,7},{40,8},{41... | collective-permute-start | bytes 393224 | tf_op jit(solution)/shard_map/ppermute | solution.py:16
  1960.8 2.8 copy-start
Sparse Core Ops, SparseCore 0:
  1460.4 498.0 all-reduce.2

commit v2 on v1

v2 whole, which is shorter than its diff:
```python
import math

import jax
import jax.numpy as jnp
from jax import lax
from jax.sharding import PartitionSpec as P

exact_mode = lax.Precision.HIGHEST


def body(queries, keys, values, cotangent, residues, decays):
    n_dp = lax.axis_size("dp")
    n_ctx = lax.axis_size("ctx")
    ctx_at = lax.axis_index("ctx")
    seq_count, channels, chunk = keys.shape
    block, order = residues.shape
    length = chunk * n_ctx
    f32 = jnp.float32

    own = jnp.concatenate([residues, decays], axis=1)
    part = lax.all_to_all(
        jnp.broadcast_to(own[None], (n_ctx,) + own.shape), "ctx", 0, 0, tiled=True
    )
    params = lax.all_to_all(
        jnp.broadcast_to(part[None], (n_dp,) + part.shape), "dp", 0, 0, tiled=True
    ).reshape(channels, 2 * order)
    dec = params[:, order:]
    scale = jnp.sqrt(1.0 - jnp.exp(-2.0 * dec / length))
    weight = params[:, :order] * scale

    gated_in = (keys.astype(f32) * values.astype(f32)).astype(jnp.bfloat16)
    gated_grad = (cotangent.astype(f32) * queries.astype(f32)).astype(jnp.bfloat16)
    g = gated_in[0].astype(f32)
    gg = gated_grad[0].astype(f32)

    pos = jnp.arange(chunk, dtype=f32)
    mid = chunk // 2
    dk = dec[:, :, None]
    grow = jnp.exp(dk * ((pos - mid) / length))
    shrink = jnp.exp(-dk * ((pos - mid) / length))
    upper = (pos[:, None] <= pos[None, :]).astype(f32)
    lower = (pos[:, None] >= pos[None, :]).astype(f32)

    fwd_state = shrink * jnp.einsum(
        "dnc,ct->dnt", g[:, None, :] * grow, upper, precision=exact_mode
    )
    bwd_state = grow * jnp.einsum(
        "dnc,ct->dnt", gg[:, None, :] * shrink, lower, precision=exact_mode
    )
    conv_intra = jnp.sum(weight[:, :, None] * fwd_state, axis=1)
    back_intra = jnp.sum(weight[:, :, None] * bwd_state, axis=1)
    cross_intra = jnp.sum(gg[:, None, :] * fwd_state, axis=-1)
    lead_fwd = jnp.exp(-dk * ((pos + 1) / length))
    lead_bwd = jnp.exp(-dk * ((chunk - pos) / length))
    cross_lead = jnp.sum(gg[:, None, :] * lead_fwd, axis=-1)
    end_fwd = fwd_state[:, :, chunk - 1]
    start_bwd = bwd_state[:, :, 0]

    groups = channels // (n_dp * n_ctx)
    stats = jnp.concatenate([end_fwd, start_bwd, cross_intra, cross_lead], axis=1)
    stats = stats.reshape(n_dp, n_ctx, groups, 4 * order)
    stats = lax.all_to_all(stats, "ctx", 1, 1, tiled=True)
    s_fwd = stats[..., :order]
    s_bwd = stats[..., order : 2 * order]
    c_intra = stats[..., 2 * order : 3 * order]
    c_lead = stats[..., 3 * order :]
    dec_grp = lax.dynamic_slice_in_dim(
        dec.reshape(n_dp, n_ctx, groups, order), ctx_at, 1, axis=1
    )
    here = jnp.arange(n_ctx)
    gap = (here[:, None] - here[None, :]).astype(f32)
    decay_dims = dec_grp[:, :, None, :, :]
    ahead = jnp.where(
        (gap > 0)[None, :, :, None, None],
        jnp.exp(-decay_dims * ((gap - 1.0) * (chunk / length))[None, :, :, None, None]),
        0.0,
    )
    behind = jnp.where(
        (gap < 0)[None, :, :, None, None],
        jnp.exp(-decay_dims * ((-gap - 1.0) * (chunk / length))[None, :, :, None, None]),
        0.0,
    )
    carry_fwd = jnp.sum(ahead * s_fwd[:, None], axis=2)
    carry_bwd = jnp.sum(behind * s_bwd[:, None], axis=2)
    cross_grp = jnp.sum(c_intra + carry_fwd * c_lead, axis=1)
    carries = lax.all_to_all(
        jnp.concatenate([carry_fwd, carry_bwd], axis=-1), "ctx", 1, 1, tiled=True
    ).reshape(channels, 2 * order)
    carry_fwd = carries[:, :order]
    carry_bwd = carries[:, order:]
    total = jnp.sum(lax.all_to_all(cross_grp, "dp", 0, 0, tiled=True), axis=0)

    own_scale = jnp.sqrt(1.0 - jnp.exp(-2.0 * decays / length))
    grad_residues = total * own_scale / math.sqrt(seq_count * n_dp * length)

    conv_full = conv_intra + jnp.sum((weight * carry_fwd)[:, :, None] * lead_fwd, axis=1)
    back_full = back_intra + jnp.sum((weight * carry_bwd)[:, :, None] * lead_bwd, axis=1)
    conv_f = conv_full.astype(jnp.bfloat16).astype(f32)[None]
    back_f = back_full.astype(jnp.bfloat16).astype(f32)[None]
    mixed = (queries.astype(f32) * conv_f).astype(jnp.bfloat16)
    grad_queries = (cotangent.astype(f32) * conv_f).astype(jnp.bfloat16)
    grad_keys = (back_f * values.astype(f32)).astype(jnp.bfloat16)
    grad_values = (back_f * keys.astype(f32)).astype(jnp.bfloat16)
    return (mixed, grad_queries, grad_keys, grad_values, grad_residues)


def solution(mesh):
    return jax.shard_map(
        body,
        mesh=mesh,
        in_specs=(
            P("dp", None, "ctx"),
            P("dp", None, "ctx"),
            P("dp", None, "ctx"),
            P("dp", None, "ctx"),
            P(("dp", "ctx"), None),
            P(("dp", "ctx"), None),
        ),
        out_specs=(
            P("dp", None, "ctx"),
            P("dp", None, "ctx"),
            P("dp", None, "ctx"),
            P("dp", None, "ctx"),
            P(("dp", "ctx"), None),
        ),
        check_vma=False,
    )
```

time: 1970 us -> 238 us (0.12)
  blocking collectives: 1330 us -> 0 us
  waiting for transfers between devices: 526 us -> 48.4 us
  local copies, waits for them, and re-layouts: 9.73 us -> 46.5 us
  other arithmetic: 15.4 us -> 44.6 us
    all_gather x1 -> x0, blocking collectives: 1330 us -> none  [body(): lax.all_gather(jnp.concatenate([residues, decays], axis=1), ('dp', 'ctx')...]
    unnamed x2 -> x0, waiting for transfers between devices: 493 us -> none
    all_to_all x0 -> x5, waiting for transfers between devices: none -> 48.4 us  [the longest x1 14.4 us: body(): lax.all_to_all(jnp.broadcast_to(part[None], (n_dp,) + part.shape), 'dp',...]
    all_to_all x0 -> x5, starting transfers between devices: none -> 47.8 us  [the longest x1 15 us: body(): lax.all_to_all(jnp.broadcast_to(part[None], (n_dp,) + part.shape), 'dp',...]
    ppermute x14 -> x0, starting transfers between devices: 33.5 us -> none  [shift_along(): return lax.ppermute(x, axis, perm=pairs)]
    ppermute x14 -> x0, waiting for transfers between devices: 33.2 us -> none  [shift_along(): return lax.ppermute(x, axis, perm=pairs)]
  transfers between devices with their start and end apart: 15 -> 5, of which waited for: 13 -> 5; matrix products, arithmetic and copies ran while one was open for 1% -> 7% of each run, Pallas kernels for 0% -> 0%
where the time goes in v2:
time: 238 us; the launch traced here: 234 us
  waiting for transfers between devices  48.4 us (20%)
  starting transfers between devices  47.8 us (20%)
  local copies, waits for them, and re-layouts  46.5 us (20%)
  matrix products  45.5 us (19%)
  other arithmetic  44.6 us (19%)
    dot_general x1, matrix products, body(): jnp.einsum('dnc,ct->dnt', g[:, None, :] * grow, upper, precision=exact_mode)  26.3 us
    unnamed x33, local copies, waits for them, and re-layouts  25.7 us
    dot_general x1, matrix products, body(): jnp.einsum('dnc,ct->dnt', gg[:, None, :] * shrink, lower, precision=exact...  19.3 us
    all_to_all x1, starting transfers between devices, body(): lax.all_to_all(jnp.broadcast_to(part[None], (n_dp,) + part.shape), 'dp',...  15 us
    all_to_all x1, waiting for transfers between devices, body(): lax.all_to_all(jnp.broadcast_to(part[None], (n_dp,) + part.shape), 'dp',...  14.4 us
    all_to_all x1, waiting for transfers between devices, body(): stats = lax.all_to_all(stats, 'ctx', 1, 1, tiled=True)  14.1 us
    reduce_sum x1, other arithmetic, body(): carry_fwd = jnp.sum(ahead * s_fwd[:, None], axis=2)  12.8 us
    all_to_all x1, starting transfers between devices, body(): lax.all_to_all(jnp.broadcast_to(own[None], (n_ctx,) + own.shape), 'ctx',...  12.6 us
  transfers between devices with their start and end apart: 5, of which 5 were waited for; matrix products, arithmetic and copies ran while one was open for 7% of the time, Pallas kernels for 0%

profile of v2, /device:TPU:1, one launch (start us, length us, event | category | flops | bytes accessed | tf_op | source)
XLA Modules:
  0.0 234.1 jit_solution(3402778385468140709)
XLA Ops:
  2.2 12.6 %all-to-all-start = ((f32[64,1,128]{2,1,0:T(1,128)}), f32[64,1,128]{2,1,0:T(1,128)S(1)}, u32[]{:S(2)}, u32[]{:S(2)}) async-start(f32[64,1,128]{2,1,0:T(1,128)} %reshape.175), calls=%async_computation | async-start | bytes 65536 | tf_op jit(solution)/shard_map/all_to_all | solution.py:21
  19.8 3.8 %all-to-all-done = f32[64,1,128]{2,1,0:T(1,128)S(1)} async-done(((f32[64,1,128]{2,1,0:T(1,128)}), f32[64,1,128]{2,1,0:T(1,128)S(1)}, u32[]{:S(2)}, u32[]{:S(2)}) %all-to-all-start) | async-done | bytes 32800 | tf_op jit(solution)/shard_map/all_to_all | solution.py:21
  26.0 15.0 %all-to-all-start.1 = ((f32[8,1,8192]{2,1,0:T(1,128)}), f32[8,1,8192]{2,1,0:T(1,128)S(1)}, u32[]{:S(2)}, u32[]{:S(2)}) async-start(f32[8,1,8192]{2,1,0:T(1,128)} %reshape.177), calls=%async_computation.1 | async-start | bytes 524288 | tf_op jit(solution)/shard_map/all_to_all | solution.py:24
  43.3 14.4 %all-to-all-done.1 = f32[8,1,8192]{2,1,0:T(1,128)S(1)} async-done(((f32[8,1,8192]{2,1,0:T(1,128)}), f32[8,1,8192]{2,1,0:T(1,128)S(1)}, u32[]{:S(2)}, u32[]{:S(2)}) %all-to-all-start.1) | async-done | bytes 262176 | tf_op jit(solution)/shard_map/all_to_all | solution.py:24
  59.9 1.5 copy.138
  61.3 1.7 fusion.38
  63.1 1.5 copy.171
  64.6 1.5 copy.168
  66.2 19.3 %fusion.4 = f32[2048,16,128]{0,2,1:T(8,128)S(1)} fusion(f32[2048,16]{0,1:T(8,128)S(1)} %copy.168, f32[128]{0:T(128)S(1)} %add_multiply_fusion.3, f32[2048,128]{0,1:T(8,128)} %fusion.27, f32[2048,16]{0,1:T(8,128)S(1)} %get-tuple-element.53), kind=kOutput, calls=%fused_computation.14 | convolution fusion | flops 6459244544 | bytes 18088448 | tf_op jit(solution)/shard_map/dnc,ct->dnt/dot_general | solution.py:47
  85.6 26.3 %multiply_reduce_fusion.6 = (f32[2048,16]{0,1:T(8,128)}, f32[2048,128]{0,1:T(8,128)}, f32[2048,16]{0,1:T(8,128)}, f32[2048,128]{0,1:T(8,128)}, f32[2048,16,128]{0,2,1:T(8,128)}) fusion(f32[2048,128]{0,1:T(8,128)S(1)} %copy-done.2, f32[2048,16]{0,1:T(8,128)S(1)} %get-tuple-element.52, f32[128]{0:T(128)S(1)} %add_multiply_fusion.2, ...), kind=kOutput, calls=%fused_computation.7 | convolution fusion | flops 6496403456 | bytes 38405120 | tf_op jit(solution)/shard_map/dnc,ct->dnt/dot_general | solution.py:44
  113.6 2.3 copy.149
  117.2 2.2 copy.150
  119.4 4.5 %copy_bitcast_fusion.1 = f32[64,8,4,64]{3,2,1,0:T(4,128)} fusion(f32[8,64,4,16]{3,2,1,0:T(4,128)} %bitcast.51, f32[8,64,4,16]{3,2,1,0:T(4,128)} %bitcast.49, f32[8,64,4,16]{3,2,1,0:T(4,128)} %bitcast.50, f32[8,64,4,16]{3,2,1,0:T(4,128)S(1)} %bitcast.48), kind=kLoop, calls=%fused_computation.69 | loop fusion | flops 393216 | bytes 1048576
  124.0 3.0 %reshape.179 = f32[64,1,2048]{2,1,0:T(1,128)} reshape(f32[64,8,4,64]{3,2,1,0:T(4,128)} %copy_bitcast_fusion.1) | data formatting | bytes 1048576
  126.9 10.3 %all-to-all-start.2 = ((f32[64,1,2048]{2,1,0:T(1,128)}), f32[64,1,2048]{2,1,0:T(1,128)S(1)}, u32[]{:S(2)}, u32[]{:S(2)}) async-start(f32[64,1,2048]{2,1,0:T(1,128)} %reshape.179), calls=%async_computation.2 | async-start | bytes 1048576 | tf_op jit(solution)/shard_map/all_to_all | solution.py:62
  140.4 14.1 %all-to-all-done.2 = f32[64,1,2048]{2,1,0:T(1,128)S(1)} async-done(((f32[64,1,2048]{2,1,0:T(1,128)}), f32[64,1,2048]{2,1,0:T(1,128)S(1)}, u32[]{:S(2)}, u32[]{:S(2)}) %all-to-all-start.2) | async-done | bytes 524320 | tf_op jit(solution)/shard_map/all_to_all | solution.py:62
  154.5 2.7 %reduce.2 = f32[64,2048]{1,0:T(8,128)} reduce(f32[64,1,2048]{2,1,0:T(1,128)S(1)} %all-to-all-done.2, f32[]{:T(128)} %broadcast.122), dimensions={1}, to_apply=%all_to_all.17.reduce_sub_computation | reduce | bytes 1048580 | tf_op jit(solution)/shard_map/all_to_all | solution.py:62
  157.2 1.7 reshape.180
  158.9 3.7 %fusion.36 = (f32[8,64,4,16]{3,2,0,1:T(4,128)}, f32[8,64,4,16]{3,2,0,1:T(4,128)}, f32[8,64,4,16]{3,2,0,1:T(4,128)}, f32[8,64,4,16]{3,2,0,1:T(4,128)}) fusion(f32[8,64,4,64]{3,2,0,1:T(4,128)S(1)} %bitcast.44), kind=kLoop, calls=%fused_computation.64 | loop fusion | bytes 1048576 | tf_op jit(solution)/shard_map/slice | solution.py:65
  162.6 1.8 copy.153
  164.4 2.5 %copy.152 = f32[8,64,4,16]{1,3,2,0:T(8,128)} copy(f32[8,64,4,16]{3,2,0,1:T(4,128)} %get-tuple-element.45) | data formatting | bytes 262144 | tf_op jit(solution)/shard_map/slice | solution.py:63
  166.8 12.8 %multiply_reduce_fusion.4 = (f32[8,64,4,16]{3,2,1,0:T(4,128)S(1)}, f32[8,64,4,16]{3,2,1,0:T(4,128)}) fusion(f32[8,64,4,16]{1,3,2,0:T(8,128)} %copy.152, f32[64,64]{1,0:T(8,128)} %add_multiply_fusion.1, f32[8,4,16]{2,1,0:T(4,128)S(1)} %negate_bitcast_fusion, pred[64,64]{1,0:T(8,128)(4,1)} %convert_compare_fusion.1, f32[8,64,4,16]{1,3,2,0:T(8,128)S(1)} %copy.153, ...), kind=kLoop, calls=%fused_computation.4 | loop fusion | flops 16711680 | bytes 567296 | tf_op jit(solution)/shard_map/reduce_sum | solution.py:83
  179.6 2.6 %fusion.23 = f32[8,4,16]{2,1,0:T(4,128)} fusion(f32[8,64,4,16]{3,2,1,0:T(4,128)S(1)} %get-tuple-element.36, f32[8,64,4,16]{3,2,0,1:T(4,128)} %get-tuple-element.43, f32[8,64,4,16]{3,2,0,1:T(4,128)} %get-tuple-element.42), kind=kLoop, calls=%fused_computation.39 | loop fusion | flops 97792 | bytes 395264 | tf_op jit(solution)/shard_map/reduce_sum | solution.py:85
  182.2 5.2 %all-to-all-start.4 = ((f32[8,4,16]{2,1,0:T(4,128)}), f32[8,4,16]{2,1,0:T(4,128)S(1)}, u32[]{:S(2)}, u32[]{:S(2)}) async-start(f32[8,4,16]{2,1,0:T(4,128)} %fusion.23), calls=%async_computation.4 | async-start | bytes 32768 | tf_op jit(solution)/shard_map/all_to_all | solution.py:91
  187.3 2.8 %copy_bitcast_fusion = f32[64,8,4,32]{3,2,1,0:T(4,128)} fusion(f32[8,64,4,16]{3,2,1,0:T(4,128)} %get-tuple-element.37, f32[8,64,4,16]{3,2,1,0:T(4,128)S(1)} %get-tuple-element.36), kind=kLoop, calls=%fused_computation.68 | loop fusion | flops 65536 | bytes 524288
  190.2 2.6 %reshape.181 = f32[64,1,1024]{2,1,0:T(1,128)} reshape(f32[64,8,4,32]{3,2,1,0:T(4,128)} %copy_bitcast_fusion) | data formatting | bytes 524288
  192.8 6.5 %all-to-all-done.4 = f32[8,4,16]{2,1,0:T(4,128)S(1)} async-done(((f32[8,4,16]{2,1,0:T(4,128)}), f32[8,4,16]{2,1,0:T(4,128)S(1)}, u32[]{:S(2)}, u32[]{:S(2)}) %all-to-all-start.4) | async-done | bytes 2080 | tf_op jit(solution)/shard_map/all_to_all | solution.py:91
  199.2 4.9 %all-to-all-start.3 = ((f32[64,1,1024]{2,1,0:T(1,128)}), f32[64,1,1024]{2,1,0:T(1,128)S(1)}, u32[]{:S(2)}, u32[]{:S(2)}) async-start(f32[64,1,1024]{2,1,0:T(1,128)} %reshape.181), calls=%async_computation.3 | async-start | bytes 524288 | tf_op jit(solution)/shard_map/all_to_all | solution.py:86
  205.4 9.6 %all-to-all-done.3 = f32[64,1,1024]{2,1,0:T(1,128)S(1)} async-done(((f32[64,1,1024]{2,1,0:T(1,128)}), f32[64,1,1024]{2,1,0:T(1,128)S(1)}, u32[]{:S(2)}, u32[]{:S(2)}) %all-to-all-start.3) | async-done | bytes 262176 | tf_op jit(solution)/shard_map/all_to_all | solution.py:86
  218.2 1.5 copy.172
  220.1 7.0 %multiply_reduce_fusion = (f32[2048,128]{0,1:T(8,128)S(1)}, f32[2048,128]{0,1:T(8,128)S(1)}) fusion(f32[128]{0:T(128)S(1)} %subtract_multiply_fusion, f32[2048,16]{0,1:T(8,128)S(1)} %get-tuple-element.51, f32[2048,16]{0,1:T(8,128)} %copy-done.4, f32[128]{0:T(128)} %copy-done.5, f32[2048,16]{0,1:T(8,128)S(1)} %get-tuple-element.50), kind=kLoop, calls=%fused_computation | loop fusion | flops 24641536 | bytes 2491392 | tf_op jit(solution)/shard_map/reduce_sum | solution.py:97
  229.7 2.0 copy.162
  (56 shorter events, 29.3 us)
Async XLA Ops:
  2.2 21.4 %all-to-all-start = ((f32[64,1,128]{2,1,0:T(1,128)}), f32[64,1,128]{2,1,0:T(1,128)S(1)}, u32[]{:S(2)}, u32[]{:S(2)}) async-start(f32[64,1,128]{2,1,0:T(1,128)} %reshape.175), calls=%async_computation | async-start | bytes 65536 | tf_op jit(solution)/shard_map/all_to_all | solution.py:21
  19.8 65.8 %copy-start.5 = (f32[128]{0:T(128)}, f32[128]{0:T(128)S(1)}, u32[]{:S(2)}) copy-start(f32[128]{0:T(128)S(1)} %add_multiply_fusion.2) | copy-start | bytes 1540
  26.0 31.7 %all-to-all-start.1 = ((f32[8,1,8192]{2,1,0:T(1,128)}), f32[8,1,8192]{2,1,0:T(1,128)S(1)}, u32[]{:S(2)}, u32[]{:S(2)}) async-start(f32[8,1,8192]{2,1,0:T(1,128)} %reshape.177), calls=%async_computation.1 | async-start | bytes 524288 | tf_op jit(solution)/shard_map/all_to_all | solution.py:24
  66.2 19.4 %copy-start.4 = (f32[2048,16]{0,1:T(8,128)}, f32[2048,16]{0,1:T(8,128)S(1)}, u32[]{:S(2)}) copy-start(f32[2048,16]{0,1:T(8,128)S(1)} %get-tuple-element.53) | copy-start | bytes 393220
  66.2 19.4 %copy-start.2 = (f32[2048,128]{0,1:T(8,128)S(1)}, f32[2048,128]{0,1:T(8,128)}, u32[]{:S(2)}) copy-start(f32[2048,128]{0,1:T(8,128)} %fusion.27) | copy-start | bytes 3145732
  66.2 19.4 %copy-start.3 = (f32[2048,128]{0,1:T(8,128)S(1)}, f32[2048,128]{0,1:T(8,128)}, u32[]{:S(2)}) copy-start(f32[2048,128]{0,1:T(8,128)} %fusion.29) | copy-start | bytes 3145732
  126.9 27.6 %all-to-all-start.2 = ((f32[64,1,2048]{2,1,0:T(1,128)}), f32[64,1,2048]{2,1,0:T(1,128)S(1)}, u32[]{:S(2)}, u32[]{:S(2)}) async-start(f32[64,1,2048]{2,1,0:T(1,128)} %reshape.179), calls=%async_computation.2 | async-start | bytes 1048576 | tf_op jit(solution)/shard_map/all_to_all | solution.py:62
  182.2 17.0 %all-to-all-start.4 = ((f32[8,4,16]{2,1,0:T(4,128)}), f32[8,4,16]{2,1,0:T(4,128)S(1)}, u32[]{:S(2)}, u32[]{:S(2)}) async-start(f32[8,4,16]{2,1,0:T(4,128)} %fusion.23), calls=%async_computation.4 | async-start | bytes 32768 | tf_op jit(solution)/shard_map/all_to_all | solution.py:91
  199.2 15.8 %all-to-all-start.3 = ((f32[64,1,1024]{2,1,0:T(1,128)}), f32[64,1,1024]{2,1,0:T(1,128)S(1)}, u32[]{:S(2)}, u32[]{:S(2)}) async-start(f32[64,1,1024]{2,1,0:T(1,128)} %reshape.181), calls=%async_computation.3 | async-start | bytes 524288 | tf_op jit(solution)/shard_map/all_to_all | solution.py:86
  220.0 7.1 %copy-start = (f32[2048,128]{0,1:T(8,128)S(1)}, f32[2048,128]{0,1:T(8,128)}, u32[]{:S(2)}) copy-start(f32[2048,128]{0,1:T(8,128)} %get-tuple-element.31) | copy-start | bytes 3145732
  220.1 7.1 %copy-start.1 = (f32[2048,128]{0,1:T(8,128)S(1)}, f32[2048,128]{0,1:T(8,128)}, u32[]{:S(2)}) copy-start(f32[2048,128]{0,1:T(8,128)} %get-tuple-element.33) | copy-start | bytes 3145732
